TPU v7x, 32 devices: a whole 2x2x4 slice. The times are simulated.
32 devices in a mesh: view: 4 (over z), brick: 8 (over y, x, core).
Axes of the slice: x: 2, y: 2, z: 4, core: 2. Of those that a mesh axis runs over, the one named last changes fastest.
Arguments:
- estimate: float32 [16, 16, 64, 256], P('brick'), may hold values from 0.5 to 2
- views_data: bfloat16 [4, 8, 112, 32, 128], P('view', 'brick'), may hold values from 0.5 to 2
- psf_taps: float32 [4, 3, 31], P('view'), may hold values from 0.02 to 1
- seg_owner: int32 [4, 8, 32, 1], P('view', 'brick'), may hold values from 0 to 7; in each aligned block of 32 rows (0 to 31, 32 to 63, ..., all dimensions but the last counted through in order) at most 8 rows name the same one
- seg_local: int32 [4, 8, 32], P('view', 'brick'), may hold values from 0 to 1
- seg_offset: int32 [4, 8, 32], P('view', 'brick'), may hold values from 0 to 12
- seg_extent: int32 [4, 8, 32], P('view', 'brick'), may hold values from 1 to 4, 112 in all within a row
- view_shift: int32 [4, 2], P('view'), may hold values from 0 to 32
Outputs:
- joined: float32 [16, 16, 64, 256], P('brick')
Inputs may be any that keep to these rules, and one draw needn't show every extreme that they name: `seg_owner`: within one tile's 32 segments no owner is named more than 8 times, and in every draw some tile names one owner exactly 8 times. `seg_extent`: the 32 extents of a tile sum to 112, and some extent is exactly 4.
All inputs are finite; a program needn't handle non-finite values.
Results may differ from a plain program's by a relative error of at most 0.0003.
Values may be sent and summed in bfloat16 or wider, within the bound.
No kernel may reach another device: no remote copies, remote signals or barrier semaphores. Data moves between devices by JAX's collectives and lax.ppermute only.
A program may use at most 128 MiB of HBM per device.

v0:
```python
import jax
import jax.numpy as jnp
from jax import lax
from jax.sharding import PartitionSpec as P

ITERS = 2
EXTMAX = 4


def blur_matrix(tap_values, length):
    centre = tap_values.shape[0] // 2
    positions = jnp.arange(length, dtype=jnp.int32)
    offsets_tab = positions[:, None] - positions[None, :] + centre
    match_table = (
        offsets_tab[:, :, None] == jnp.arange(tap_values.shape[0], dtype=jnp.int32)[None, None, :]
    ).astype(tap_values.dtype)
    return jnp.sum(match_table * tap_values[None, None, :], axis=-1)


def apply_blur(volume, matrices):
    along_z, along_y, along_x = matrices
    highest = lax.Precision.HIGHEST
    volume = jnp.einsum("...xyz,zw->...xyw", volume, along_z, precision=highest)
    volume = jnp.einsum("...xyz,yw->...xwz", volume, along_y, precision=highest)
    volume = jnp.einsum("...xyz,xw->...wyz", volume, along_x, precision=highest)
    return volume


def view_matrices(view_taps, tile_x, tile_y, tile_z):
    normed = view_taps / jnp.sum(view_taps, axis=1, keepdims=True)
    forward = (
        blur_matrix(normed[2], tile_z),
        blur_matrix(normed[1], tile_y),
        blur_matrix(normed[0], tile_x),
    )
    backward = (forward[0].T, forward[1].T, forward[2].T)
    return (forward, backward)


def slot_ranks(owners):
    positions = jnp.arange(owners.shape[-1], dtype=jnp.int32)
    same_owner = owners[..., :, None] == owners[..., None, :]
    earlier = positions[None, :] < positions[:, None]
    return jnp.sum((same_owner & earlier).astype(jnp.int32), axis=-1)


def on_device(
    estimate, views_data, psf_taps, seg_owner, seg_local, seg_offset, seg_extent, view_shift
):
    per_owner, brick_x, brick_y, brick_z = estimate.shape
    tile_x, tile_y, tile_z = (views_data.shape[2], views_data.shape[3], views_data.shape[4])
    seg_count = seg_extent.shape[2]
    brick_count = lax.axis_size("brick")
    owner_me = lax.axis_index("brick")
    capacity = max(2, 2 * seg_count // brick_count)
    slot_rows = capacity * EXTMAX
    own_rows = per_owner * brick_x
    forward, backward = view_matrices(psf_taps[0], tile_x, tile_y, tile_z)
    shift_y = view_shift[0, 0]
    shift_z = view_shift[0, 1]
    measured = views_data[0, 0].astype(jnp.float32)
    lists = (
        lax.all_gather(seg_owner[:, :, :, 0], "brick", axis=1, tiled=True),
        lax.all_gather(seg_local, "brick", axis=1, tiled=True),
        lax.all_gather(seg_offset, "brick", axis=1, tiled=True),
        lax.all_gather(seg_extent, "brick", axis=1, tiled=True),
    )
    all_owner, all_local, all_offset, all_extent = (
        lists[0][0],
        lists[1][0],
        lists[2][0],
        lists[3][0],
    )
    own_owner = seg_owner[0, 0, :, 0]
    own_local = seg_local[0, 0]
    own_offset = seg_offset[0, 0]
    own_extent = seg_extent[0, 0]
    own_rank = slot_ranks(own_owner)
    seg_ids = jnp.arange(seg_count, dtype=jnp.int32)
    peer_ids = jnp.arange(brick_count, dtype=jnp.int32)
    slot_ids = jnp.arange(capacity, dtype=jnp.int32)
    row_steps = jnp.arange(EXTMAX, dtype=jnp.int32)
    starts = jnp.cumsum(own_extent) - own_extent
    tile_rows = jnp.arange(tile_x, dtype=jnp.int32)
    seg_of = jnp.sum((starts[None, :] <= tile_rows[:, None]).astype(jnp.int32), axis=1) - 1
    within = tile_rows - starts[seg_of]
    source_of_row = (
        (own_owner[seg_of] * per_owner + own_local[seg_of]) * brick_x + own_offset[seg_of] + within
    )
    back_match = (own_owner[None, None, :] == peer_ids[:, None, None]) & (
        own_rank[None, None, :] == slot_ids[None, :, None]
    )
    back_valid = jnp.any(back_match, axis=-1)
    back_seg = jnp.sum(back_match.astype(jnp.int32) * seg_ids, axis=-1)
    back_mask = back_valid[:, :, None] & (
        row_steps[None, None, :] < own_extent[back_seg][:, :, None]
    )
    back_rows = jnp.where(
        back_mask, starts[back_seg][:, :, None] + row_steps[None, None, :], 0
    ).reshape(-1)
    back_mask = back_mask.reshape(-1)
    all_rank = slot_ranks(all_owner)
    owner_match = (all_owner[:, None, :] == owner_me) & (
        all_rank[:, None, :] == slot_ids[None, :, None]
    )
    owner_valid = jnp.any(owner_match, axis=-1)
    owner_seg = jnp.sum(owner_match.astype(jnp.int32) * seg_ids, axis=-1)
    owner_base = jnp.take_along_axis(all_local, owner_seg, axis=1) * brick_x + jnp.take_along_axis(
        all_offset, owner_seg, axis=1
    )
    owner_ext = jnp.take_along_axis(all_extent, owner_seg, axis=1)
    owner_mask = owner_valid[:, :, None] & (row_steps[None, None, :] < owner_ext[:, :, None])
    owner_rows = jnp.where(
        owner_mask, owner_base[:, :, None] + row_steps[None, None, :], 0
    ).reshape(-1)
    owner_mask = owner_mask.reshape(-1)
    landing = (
        (owner_rows[None, :] == jnp.arange(own_rows, dtype=jnp.int32)[:, None])
        & owner_mask[None, :]
    ).astype(jnp.float32)

    def to_owners(projected):
        outgoing = jnp.where(back_mask[:, None, None], jnp.take(projected, back_rows, axis=0), 0.0)
        outgoing = outgoing.reshape(brick_count, slot_rows, tile_y, tile_z)
        arrived = lax.all_to_all(
            outgoing, "brick", split_axis=0, concat_axis=0, tiled=True
        ).reshape(-1, tile_y, tile_z)
        accumulated = jnp.einsum("pq,qyz->pyz", landing, arrived, precision=lax.Precision.HIGHEST)
        brick_part = lax.dynamic_update_slice(
            jnp.zeros((own_rows, brick_y, brick_z), jnp.float32), accumulated, (0, shift_y, shift_z)
        )
        brick_part = brick_part.reshape(per_owner, brick_x, brick_y, brick_z)
        return lax.psum(brick_part, "view")

    weight = to_owners(apply_blur(jnp.ones((tile_x, tile_y, tile_z), jnp.float32), backward))
    current = estimate
    for sweep in range(ITERS):
        flat_est = current.reshape(own_rows, brick_y, brick_z)
        cropped = lax.dynamic_slice(
            flat_est, (0, shift_y, shift_z), (own_rows, tile_y, tile_z)
        ).astype(jnp.bfloat16)
        gathered = lax.all_gather(cropped, "brick", axis=0, tiled=True)
        view_tile = jnp.take(gathered, source_of_row, axis=0)
        correction_view_tile = view_tile.astype(jnp.float32)
        quotient = measured / apply_blur(correction_view_tile, forward)
        correction = to_owners(apply_blur(quotient, backward))
        current = current * (1.0 + correction) / (1.0 + weight)
    return current


def solution(mesh):
    placed = (
        P("brick", None, None, None),
        P("view", "brick", None, None, None),
        P("view", None, None),
        P("view", "brick", None, None),
        P("view", "brick", None),
        P("view", "brick", None),
        P("view", "brick", None),
        P("view", None),
    )
    return jax.shard_map(
        on_device,
        mesh=mesh,
        in_specs=placed,
        out_specs=P("brick", None, None, None),
        check_vma=False,
    )
```

profile of v0, /device:TPU:0, one launch (start us, length us, event | category | flops | bytes accessed | tf_op | source)
XLA Modules:
  0.0 637.1 jit_solution(17363092485871562912)
XLA Ops:
  6.5 1.3 fusion.66
  11.9 2.2 dynamic-slice_convert_fusion.1
  14.1 0.7 copy.56
  15.0 0.7 bitcast_subtract_fusion
  15.8 1.2 gather_fusion.4
  17.0 1.6 gather_fusion.1
  18.8 1.2 gather_fusion.2
  20.1 1.2 gather_fusion.3
  21.7 0.8 gather_fusion.5
  22.4 0.8 gather_fusion
  25.0 1.6 fusion.22
  26.6 1.7 convolution_bitcast_fusion.2
  28.3 2.6 fusion.6
  31.5 3.0 gather_fusion.11
  34.6 10.2 %all-gather.4.cloned.1.call-done = bf16[256,32,128]{2,1,0:T(8,128)(2,1)} async-done(((bf16[32,32,128]{2,1,0:T(8,128)(2,1)}), bf16[256,32,128]{2,1,0:T(8,128)(2,1)}) %all-gather.4.cloned.1.call-update) | async-done | bytes 2097168 | tf_op jit(solution)/shard_map/all_gather | solution.py:142
  44.8 2.3 gather_fusion.9
  47.1 0.9 fusion.20
  48.1 1.7 convolution_bitcast_fusion.4
  49.8 3.1 convert_divide_fusion.1
  52.9 2.0 fusion.10
  54.9 1.7 convolution_bitcast_fusion.3
  56.6 2.6 fusion.8
  59.9 3.0 gather_fusion.10
  62.8 16.0 %select_select_fusion.1 = (f32[256,32,128]{2,1,0:T(8,128)S(1)}, f32[256,32,128]{2,1,0:T(8,128)}) fusion(f32[256,32,128]{2,1,0:T(8,128)} %gather_fusion.11, pred[256]{0:T(512)(128)(4,1)S(1)} %get-tuple-element.12, pred[256]{0:T(512)(128)(4,1)S(1)} %and.102, f32[256,32,128]{2,1,0:T(8,128)} %gather_fusion.10), kind=kLoop, calls=%fused_computation.15 | loop fusion | flops 4194304 | bytes 16777728 | tf_op jit(solution)/shard_map/jit(_where)/select_n | solution.py:123
  78.8 4.3 copy.69
  83.2 4.5 all-to-all-start.1
  87.7 6.5 %copy.64 = f32[8,32,32,128]{3,1,2,0:T(8,128)} copy(f32[8,32,32,128]{3,2,1,0:T(8,128)} %bitcast.133) | data formatting | bytes 8388608 | tf_op jit(solution)/shard_map/reshape | solution.py:124
  94.3 42.6 %all-to-all-done.1 = f32[8,32,32,128]{3,1,2,0:T(8,128)} async-done(((f32[8,32,32,128]{3,1,2,0:T(8,128)}), f32[8,32,32,128]{3,1,2,0:T(8,128)}, u32[]{:S(2)}, u32[]{:S(2)}) %all-to-all-start.1) | async-done | bytes 4194336 | tf_op jit(solution)/shard_map/all_to_all | solution.py:125
  136.8 4.6 all-to-all-start
  141.5 52.0 %all-gather = s32[1,8,32,1]{2,3,0,1:T(1,128)S(1)} all-gather(s32[1,1,32,1]{2,3,0,1:T(1,128)S(1)} %bitcast.124), channel_id=2, replica_groups=mesh['view'=4,'brick'=8] {'brick'}, dimensions={1}, use_global_device_ids=true | all-gather | bytes 1152 | tf_op jit(solution)/shard_map/all_gather | solution.py:63
  194.1 7.9 %all_gather.20 = s32[1,8,32]{2,0,1:T(1,128)S(1)} all-gather(s32[1,1,32]{2,0,1:T(1,128)S(1)} %bitcast.126), channel_id=1, replica_groups=mesh['view'=4,'brick'=8] {'brick'}, dimensions={1}, use_global_device_ids=true | all-gather | bytes 1152 | tf_op jit(solution)/shard_map/all_gather | solution.py:64
  202.0 0.7 gather_fusion.7
  202.8 8.7 %all_gather.21 = s32[1,8,32]{2,0,1:T(1,128)S(1)} all-gather(s32[1,1,32]{2,0,1:T(1,128)S(1)} %bitcast.128), channel_id=1, replica_groups=mesh['view'=4,'brick'=8] {'brick'}, dimensions={1}, use_global_device_ids=true | all-gather | bytes 1152 | tf_op jit(solution)/shard_map/all_gather | solution.py:65
  211.5 0.7 gather_fusion.8
  212.3 7.9 %all_gather.19 = s32[1,8,32]{2,0,1:T(1,128)S(1)} all-gather(s32[1,1,32]{2,0,1:T(1,128)S(1)} %bitcast.117), channel_id=1, replica_groups=mesh['view'=4,'brick'=8] {'brick'}, dimensions={1}, use_global_device_ids=true | all-gather | bytes 1152 | tf_op jit(solution)/shard_map/all_gather | solution.py:66
  220.2 0.7 gather_fusion.6
  221.6 2.8 copy.70
  224.5 1.6 fusion.47
  226.5 2.8 copy.65
  229.3 1.6 fusion.49
  231.5 13.4 %dynamic_update_slice.10 = f32[32,64,256]{2,1,0:T(8,128)S(1)} dynamic-update-slice(f32[32,64,256]{2,1,0:T(8,128)S(1)} %broadcast.183.clone.1, f32[32,32,128]{2,1,0:T(8,128)S(1)} %copy.71, s32[]{:T(128)} %constant.39.clone.1, s32[]{:T(128)S(6)} %select_n.82, s32[]{:T(128)S(6)} %select_n.83) | dynamic-update-slice | bytes 1048580 | tf_op jit(solution)/shard_map/dynamic_update_slice | solution.py:129
  244.9 1.7 broadcast.183.clone
  246.6 13.9 %dynamic_update_slice.9 = f32[32,64,256]{2,1,0:T(8,128)} dynamic-update-slice(f32[32,64,256]{2,1,0:T(8,128)} %broadcast.183.clone, f32[32,32,128]{2,1,0:T(8,128)S(1)} %copy.66, s32[]{:T(128)} %constant.39.clone.1, s32[]{:T(128)S(6)} %select_n.82, s32[]{:T(128)S(6)} %select_n.83) | dynamic-update-slice | bytes 1048580 | tf_op jit(solution)/shard_map/dynamic_update_slice | solution.py:129
  260.6 154.2 %all-reduce.6.cloned.1.call-done = (f32[2,16,64,256]{3,2,1,0:T(8,128)}, f32[2,16,64,256]{3,2,1,0:T(8,128)}) async-done(((f32[2,16,64,256]{3,2,1,0:T(8,128)}, f32[2,16,64,256]{3,2,1,0:T(8,128)}), (f32[2,16,64,256]{3,2,1,0:T(8,128)}, f32[2,16,64,256]{3,2,1,0:T(8,128)})) %all-reduce.6.cloned.1.call-update) | async-done | bytes 4194320 | tf_op jit(solution)/shard_map/psum | solution.py:133
  414.8 3.5 multiply_divide_fusion.1
  418.2 1.3 copy-done.4
  419.5 0.9 dynamic-slice_convert_fusion
  420.7 26.6 %all-gather.6.cloned.1.call-done = bf16[256,32,128]{2,1,0:T(8,128)(2,1)} async-done(((bf16[32,32,128]{2,1,0:T(8,128)(2,1)}), bf16[256,32,128]{2,1,0:T(8,128)(2,1)}) %all-gather.6.cloned.1.call-update) | async-done | bytes 2097168 | tf_op jit(solution)/shard_map/all_gather | solution.py:142
  447.4 2.3 gather_fusion.12
  449.7 0.9 fusion.18
  450.7 1.7 convolution_bitcast_fusion.1
  452.4 2.9 convert_divide_fusion
  455.3 2.0 fusion.2
  457.3 1.7 convolution_bitcast_fusion
  459.0 2.9 fusion
  462.5 3.0 gather_fusion.13
  465.5 3.8 select_select_fusion
  469.2 2.4 copy.78
  471.6 51.6 %all_to_all.15 = f32[8,32,32,128]{3,1,2,0:T(8,128)S(1)} all-to-all(f32[8,32,32,128]{3,1,2,0:T(8,128)S(1)} %copy.78), channel_id=1, replica_groups=mesh['view'=4,'brick'=8] {'brick'}, dimensions={0} | all-to-all | bytes 8388608 | tf_op jit(solution)/shard_map/all_to_all | solution.py:125
  523.8 1.6 fusion.45
  525.8 1.5 broadcast.183
  527.3 14.1 %dynamic_update_slice.11 = f32[32,64,256]{2,1,0:T(8,128)} dynamic-update-slice(f32[32,64,256]{2,1,0:T(8,128)} %broadcast.183, f32[32,32,128]{2,1,0:T(8,128)S(1)} %copy.80, s32[]{:T(128)} %constant.39.clone.1, s32[]{:T(128)S(6)} %select_n.82, s32[]{:T(128)S(6)} %select_n.83) | dynamic-update-slice | bytes 1048580 | tf_op jit(solution)/shard_map/dynamic_update_slice | solution.py:129
  541.4 84.5 %all-reduce.4.cloned.1.call-done = f32[2,16,64,256]{3,2,1,0:T(8,128)} async-done(((f32[2,16,64,256]{3,2,1,0:T(8,128)}), f32[2,16,64,256]{3,2,1,0:T(8,128)}) %all-reduce.4.cloned.1.call-update) | async-done | bytes 2097168 | tf_op jit(solution)/shard_map/psum | solution.py:133
  625.9 4.2 multiply_divide_fusion
  (85 shorter events, 8.0 us)
Async XLA Ops:
  6.5 12.1 %copy-start.1 = (s32[1,1,32,1]{2,3,1,0:T(1,128)S(1)}, s32[1,1,32,1]{2,3,1,0:T(1,128)}, u32[]{:S(2)}) copy-start(s32[1,1,32,1]{2,3,1,0:T(1,128)} %param.17) | copy-start | bytes 388
  6.5 12.3 %copy-start.2 = (s32[1,1,32]{2,1,0:T(1,128)S(1)}, s32[1,1,32]{2,1,0:T(1,128)}, u32[]{:S(2)}) copy-start(s32[1,1,32]{2,1,0:T(1,128)} %param.18) | copy-start | bytes 388
  6.5 13.5 %copy-start.3 = (s32[1,1,32]{2,1,0:T(1,128)S(1)}, s32[1,1,32]{2,1,0:T(1,128)}, u32[]{:S(2)}) copy-start(s32[1,1,32]{2,1,0:T(1,128)} %param.19) | copy-start | bytes 388
  6.5 38.2 %all-gather.4.cloned.1.call-start = ((), (), s32[]{:S(2)}) async-start(), calls=%async_computation.3 | async-start | bytes 2359296 | tf_op jit(solution)/shard_map/all_gather | solution.py:142
  21.6 0.8 copy-start
  22.4 1.6 copy-start.7
  48.1 1.7 copy-start.8
  83.2 53.6 %all-to-all-start.1 = ((f32[8,32,32,128]{3,1,2,0:T(8,128)}), f32[8,32,32,128]{3,1,2,0:T(8,128)}, u32[]{:S(2)}, u32[]{:S(2)}) async-start(f32[8,32,32,128]{3,1,2,0:T(8,128)} %copy.69), calls=%async_computation.1 | async-start | bytes 8388608 | tf_op jit(solution)/shard_map/all_to_all | solution.py:125
  136.8 89.6 %all-to-all-start = ((f32[8,32,32,128]{3,1,2,0:T(8,128)}), f32[8,32,32,128]{3,1,2,0:T(8,128)}, u32[]{:S(2)}, u32[]{:S(2)}) async-start(f32[8,32,32,128]{3,1,2,0:T(8,128)} %copy.64), calls=%async_computation | async-start | bytes 8388608 | tf_op jit(solution)/shard_map/all_to_all | solution.py:125
  141.4 273.3 %all-reduce.6.cloned.1.call-start = ((), (), s32[]{:S(2)}) async-start(), calls=%async_computation.6 | async-start | bytes 8388608 | tf_op jit(solution)/shard_map/psum | solution.py:133
  244.9 15.6 %copy-start.6 = (f32[32,64,256]{2,1,0:T(8,128)}, f32[32,64,256]{2,1,0:T(8,128)S(1)}, u32[]{:S(2)}) copy-start(f32[32,64,256]{2,1,0:T(8,128)S(1)} %dynamic_update_slice.10) | copy-start | bytes 6291460
  260.5 186.9 %all-gather.6.cloned.1.call-start = ((), (), s32[]{:S(2)}) async-start(), calls=%async_computation.4 | async-start | bytes 2359296 | tf_op jit(solution)/shard_map/all_gather | solution.py:142
  418.2 1.3 copy-start.4
  420.5 205.4 %all-reduce.4.cloned.1.call-start = ((), (), s32[]{:S(2)}) async-start(), calls=%async_computation.5 | async-start | bytes 4194304 | tf_op jit(solution)/shard_map/psum | solution.py:133
  450.7 1.7 copy-start.9
  527.3 98.5 %copy-start.5 = (f32[2,16,64,256]{3,2,1,0:T(8,128)S(1)}, f32[2,16,64,256]{3,2,1,0:T(8,128)}, u32[]{:S(2)}) copy-start(f32[2,16,64,256]{3,2,1,0:T(8,128)} %copy-done.4) | copy-start | bytes 6291460
Sparse Core Ops, SparseCore 0:
  14.2 30.5 all-gather.3
  260.6 154.0 all-reduce.5
  420.6 26.7 all-gather.5
  541.5 84.2 all-reduce.3
where the time goes:
time: 648 us; the launch traced here: 637 us
  waiting for transfers between devices  318 us (49%)
  blocking collectives  128 us (20%)
  local copies, waits for them, and re-layouts  97.2 us (15%)
  matrix products  35 us (5%)
  other arithmetic  31.1 us (5%)
  between operations  18.1 us (3%)
  starting transfers between devices  9.48 us (1%)
    psum x2, waiting for transfers between devices, to_owners(): return lax.psum(brick_part, 'view')  239 us
    all_gather x1, blocking collectives, on_device(): lax.all_gather(seg_owner[:, :, :, 0], 'brick', axis=1, tiled=True)  52 us
    all_to_all x1, blocking collectives, to_owners(): lax.all_to_all(outgoing, 'brick', split_axis=0, concat_axis=0, tiled=True)  51.6 us
    all_to_all x2, waiting for transfers between devices, to_owners(): lax.all_to_all(outgoing, 'brick', split_axis=0, concat_axis=0, tiled=True)  42.6 us
    dynamic_update_slice x3, local copies, waits for them, and re-layouts, to_owners(): lax.dynamic_update_slice(jnp.zeros((own_rows, brick_y, brick_z), jnp.floa...  41.3 us
    all_gather x2, waiting for transfers between devices, on_device(): gathered = lax.all_gather(cropped, 'brick', axis=0, tiled=True)  36.9 us
    select_n x2, other arithmetic, to_owners(): jnp.where(back_mask[:, None, None], jnp.take(projected, back_rows, axis=0...  19.7 us
    dot_general x5, matrix products, apply_blur(): volume = jnp.einsum('...xyz,xw->...wyz', volume, along_x, precision=highest)  14.2 us
  transfers between devices with their start and end apart: 6, of which 5 were waited for; matrix products, arithmetic and copies ran while one was open for 6% of the time, Pallas kernels for 0%

commit v1 on v0

--- a/solution.py
+++ b/solution.py
@@ -130,7 +130,7 @@
             jnp.zeros((own_rows, brick_y, brick_z), jnp.float32), accumulated, (0, shift_y, shift_z)
         )
         brick_part = brick_part.reshape(per_owner, brick_x, brick_y, brick_z)
-        return lax.psum(brick_part, "view")
+        return jnp.sum(lax.all_gather(brick_part, "view"), axis=0)
 
     weight = to_owners(apply_blur(jnp.ones((tile_x, tile_y, tile_z), jnp.float32), backward))
     current = estimate

time: 648 us -> 788 us (1.22)
  waiting for transfers between devices: 318 us -> 403 us
  blocking collectives: 128 us -> 180 us
  other arithmetic: 31.1 us -> 41.3 us
    all_gather x0 -> x3, waiting for transfers between devices: none -> 368 us  [to_owners(): return jnp.sum(lax.all_gather(brick_part, 'view'), axis=0)]
    psum x2 -> x0, waiting for transfers between devices: 239 us -> none  [to_owners(): return lax.psum(brick_part, 'view')]
    all_to_all x1 -> x2, blocking collectives: 51.6 us -> 103 us  [to_owners(): lax.all_to_all(outgoing, 'brick', split_axis=0, concat_axis=0, tiled=True)]
    all_to_all x2 -> x1, waiting for transfers between devices: 42.6 us -> 0.01 us  [to_owners(): lax.all_to_all(outgoing, 'brick', split_axis=0, concat_axis=0, tiled=True)]
    reduce_sum x0 -> x3, other arithmetic: none -> 15.9 us  [to_owners(): return jnp.sum(lax.all_gather(brick_part, 'view'), axis=0)]
    select_n x2, other arithmetic: 19.7 us -> 9.95 us  [to_owners(): jnp.where(back_mask[:, None, None], jnp.take(projected, back_rows, axis=0...]
where the time goes in v1:
time: 788 us; the launch traced here: 777 us
  waiting for transfers between devices  403 us (51%)
  blocking collectives  180 us (23%)
  local copies, waits for them, and re-layouts  95.8 us (12%)
  other arithmetic  41.3 us (5%)
  matrix products  34.5 us (4%)
  between operations  18.2 us (2%)
    all_gather x3, waiting for transfers between devices, to_owners(): return jnp.sum(lax.all_gather(brick_part, 'view'), axis=0)  368 us
    all_to_all x2, blocking collectives, to_owners(): lax.all_to_all(outgoing, 'brick', split_axis=0, concat_axis=0, tiled=True)  103 us
    all_gather x1, blocking collectives, on_device(): lax.all_gather(seg_owner[:, :, :, 0], 'brick', axis=1, tiled=True)  51.9 us
    dynamic_update_slice x3, local copies, waits for them, and re-layouts, to_owners(): lax.dynamic_update_slice(jnp.zeros((own_rows, brick_y, brick_z), jnp.floa...  40.1 us
    all_gather x2, waiting for transfers between devices, on_device(): gathered = lax.all_gather(cropped, 'brick', axis=0, tiled=True)  34.8 us
    reduce_sum x3, other arithmetic, to_owners(): return jnp.sum(lax.all_gather(brick_part, 'view'), axis=0)  15.9 us
  transfers between devices with their start and end apart: 6, of which 5 were waited for; matrix products, arithmetic and copies ran while one was open for 6% of the time, Pallas kernels for 0%

profile of v1, /device:TPU:0, one launch (start us, length us, event | category | flops | bytes accessed | tf_op | source)
XLA Modules:
  0.0 777.3 jit_solution(4650851245382766486)
XLA Ops:
  6.5 1.3 fusion.70
  11.9 2.2 dynamic-slice_convert_fusion
  15.8 1.2 gather_fusion.4
  17.0 1.6 gather_fusion.1
  18.6 0.9 convert_reduce_fusion.2
  20.2 1.2 gather_fusion.2
  21.4 1.2 gather_fusion.3
  23.8 0.8 gather_fusion
  26.3 1.6 fusion.26
  27.9 1.7 convolution_bitcast_fusion.2
  29.6 2.6 fusion.10
  32.9 3.0 gather_fusion.11
  35.9 8.9 %all-gather.7.cloned.1.call-done = bf16[256,32,128]{2,1,0:T(8,128)(2,1)} async-done(((bf16[32,32,128]{2,1,0:T(8,128)(2,1)}), bf16[256,32,128]{2,1,0:T(8,128)(2,1)}) %all-gather.7.cloned.1.call-update) | async-done | bytes 2097168 | tf_op jit(solution)/shard_map/all_gather | solution.py:142
  44.8 2.3 gather_fusion.9
  47.1 0.9 fusion.24
  48.1 1.7 convolution_bitcast_fusion.4
  49.8 3.1 convert_divide_fusion.1
  52.9 2.0 fusion.14
  54.9 1.7 convolution_bitcast_fusion.3
  56.5 2.6 fusion.12
  59.8 3.0 gather_fusion.10
  62.8 6.2 select_select_fusion.1
  68.9 4.3 copy.71
  73.3 4.7 all-to-all-start.1
  78.1 51.9 %all-gather = s32[1,8,32,1]{2,3,0,1:T(1,128)S(1)} all-gather(s32[1,1,32,1]{2,3,0,1:T(1,128)S(1)} %bitcast.124), channel_id=2, replica_groups=mesh['view'=4,'brick'=8] {'brick'}, dimensions={1}, use_global_device_ids=true | all-gather | bytes 1152 | tf_op jit(solution)/shard_map/all_gather | solution.py:63
  130.6 7.9 %all_gather.29 = s32[1,8,32]{2,0,1:T(1,128)S(1)} all-gather(s32[1,1,32]{2,0,1:T(1,128)S(1)} %bitcast.126), channel_id=1, replica_groups=mesh['view'=4,'brick'=8] {'brick'}, dimensions={1}, use_global_device_ids=true | all-gather | bytes 1152 | tf_op jit(solution)/shard_map/all_gather | solution.py:64
  139.3 8.7 %all_gather.30 = s32[1,8,32]{2,0,1:T(1,128)S(1)} all-gather(s32[1,1,32]{2,0,1:T(1,128)S(1)} %bitcast.128), channel_id=1, replica_groups=mesh['view'=4,'brick'=8] {'brick'}, dimensions={1}, use_global_device_ids=true | all-gather | bytes 1152 | tf_op jit(solution)/shard_map/all_gather | solution.py:65
  148.8 7.9 %all_gather.28 = s32[1,8,32]{2,0,1:T(1,128)S(1)} all-gather(s32[1,1,32]{2,0,1:T(1,128)S(1)} %bitcast.117), channel_id=1, replica_groups=mesh['view'=4,'brick'=8] {'brick'}, dimensions={1}, use_global_device_ids=true | all-gather | bytes 1152 | tf_op jit(solution)/shard_map/all_gather | solution.py:66
  158.2 2.8 copy.72
  161.1 1.6 fusion.51
  163.3 13.4 %dynamic_update_slice.10 = f32[32,64,256]{2,1,0:T(8,128)S(1)} dynamic-update-slice(f32[32,64,256]{2,1,0:T(8,128)S(1)} %broadcast.183.clone.1, f32[32,32,128]{2,1,0:T(8,128)S(1)} %copy.73, s32[]{:T(128)} %constant.39.clone.1, s32[]{:T(128)S(6)} %select_n.82, s32[]{:T(128)S(6)} %select_n.83) | dynamic-update-slice | bytes 1048580 | tf_op jit(solution)/shard_map/dynamic_update_slice | solution.py:129
  176.6 1.3 copy-done.8
  178.1 4.6 copy.64
  182.6 51.7 %all_to_all.15 = f32[8,32,32,128]{3,1,2,0:T(8,128)S(1)} all-to-all(f32[8,32,32,128]{3,1,2,0:T(8,128)S(1)} %copy.64), channel_id=1, replica_groups=mesh['view'=4,'brick'=8] {'brick'}, dimensions={0} | all-to-all | bytes 8388608 | tf_op jit(solution)/shard_map/all_to_all | solution.py:125
  235.0 1.6 fusion.53
  237.2 13.4 %dynamic_update_slice.9 = f32[32,64,256]{2,1,0:T(8,128)S(1)} dynamic-update-slice(f32[32,64,256]{2,1,0:T(8,128)S(1)} %broadcast.183.clone, f32[32,32,128]{2,1,0:T(8,128)S(1)} %copy.66, s32[]{:T(128)} %constant.39.clone.1, s32[]{:T(128)S(6)} %select_n.82, s32[]{:T(128)S(6)} %select_n.83) | dynamic-update-slice | bytes 1048580 | tf_op jit(solution)/shard_map/dynamic_update_slice | solution.py:129
  250.6 1.3 copy-done.9
  252.0 74.9 %all-gather.11.cloned.1.call-done = f32[4,2,16,64,256]{4,3,2,1,0:T(8,128)} async-done(((f32[1,2,16,64,256]{4,3,2,1,0:T(8,128)}), f32[4,2,16,64,256]{4,3,2,1,0:T(8,128)}) %all-gather.11.cloned.1.call-update) | async-done | bytes 8388624 | tf_op jit(solution)/shard_map/all_gather | solution.py:133
  326.8 4.4 reduce_sum.121
  331.3 145.0 %all-gather.9.cloned.1.call-done = f32[4,2,16,64,256]{4,3,2,1,0:T(8,128)} async-done(((f32[1,2,16,64,256]{4,3,2,1,0:T(8,128)}), f32[4,2,16,64,256]{4,3,2,1,0:T(8,128)}) %all-gather.9.cloned.1.call-update) | async-done | bytes 8388624 | tf_op jit(solution)/shard_map/all_gather | solution.py:133
  476.2 5.7 reduce_sum.120
  482.0 5.7 fusion.3
  487.7 1.3 copy-done.6
  489.2 0.8 copy.138
  490.3 25.9 %all-gather.13.cloned.1.call-done = bf16[256,32,128]{2,1,0:T(8,128)(2,1)} async-done(((bf16[32,32,128]{2,1,0:T(8,128)(2,1)}), bf16[256,32,128]{2,1,0:T(8,128)(2,1)}) %all-gather.13.cloned.1.call-update) | async-done | bytes 2097168 | tf_op jit(solution)/shard_map/all_gather | solution.py:142
  516.1 2.3 gather_fusion.12
  518.5 0.9 fusion.22
  519.4 1.7 convolution_bitcast_fusion.1
  521.1 2.9 convert_divide_fusion
  524.0 2.0 fusion.6
  526.0 1.7 convolution_bitcast_fusion
  527.7 2.6 fusion.4
  530.3 0.8 copy.81
  531.1 3.0 gather_fusion.13
  534.1 3.8 select_select_fusion
  537.9 2.4 copy.82
  540.3 51.6 %all_to_all.16 = f32[8,32,32,128]{3,1,2,0:T(8,128)S(1)} all-to-all(f32[8,32,32,128]{3,1,2,0:T(8,128)S(1)} %copy.82), channel_id=1, replica_groups=mesh['view'=4,'brick'=8] {'brick'}, dimensions={0} | all-to-all | bytes 8388608 | tf_op jit(solution)/shard_map/all_to_all | solution.py:125
  592.5 1.6 fusion.49
  594.7 13.4 %dynamic_update_slice.11 = f32[32,64,256]{2,1,0:T(8,128)S(1)} dynamic-update-slice(f32[32,64,256]{2,1,0:T(8,128)S(1)} %broadcast.183, f32[32,32,128]{2,1,0:T(8,128)S(1)} %copy.84, s32[]{:T(128)} %constant.39.clone.1, s32[]{:T(128)S(6)} %select_n.82, s32[]{:T(128)S(6)} %select_n.83) | dynamic-update-slice | bytes 1048580 | tf_op jit(solution)/shard_map/dynamic_update_slice | solution.py:129
  608.1 1.3 copy-done.7
  609.4 147.9 %all-gather.15.cloned.1.call-done = f32[4,2,16,64,256]{4,3,2,1,0:T(8,128)} async-done(((f32[1,2,16,64,256]{4,3,2,1,0:T(8,128)}), f32[4,2,16,64,256]{4,3,2,1,0:T(8,128)}) %all-gather.15.cloned.1.call-update) | async-done | bytes 8388624 | tf_op jit(solution)/shard_map/all_gather | solution.py:133
  757.3 5.7 reduce_sum.122
  763.0 4.7 fusion.1
  767.8 2.5 copy.86
  (98 shorter events, 13.5 us)
Async XLA Ops:
  6.5 13.7 %copy-start.2 = (s32[1,1,32]{2,1,0:T(1,128)S(1)}, s32[1,1,32]{2,1,0:T(1,128)}, u32[]{:S(2)}) copy-start(s32[1,1,32]{2,1,0:T(1,128)} %param.18) | copy-start | bytes 388
  6.5 14.9 %copy-start.3 = (s32[1,1,32]{2,1,0:T(1,128)S(1)}, s32[1,1,32]{2,1,0:T(1,128)}, u32[]{:S(2)}) copy-start(s32[1,1,32]{2,1,0:T(1,128)} %param.19) | copy-start | bytes 388
  6.5 38.2 %all-gather.7.cloned.1.call-start = ((), (), s32[]{:S(2)}) async-start(), calls=%async_computation.3 | async-start | bytes 2359296 | tf_op jit(solution)/shard_map/all_gather | solution.py:142
  23.0 0.8 copy-start
  23.8 1.6 copy-start.10
  48.1 1.7 copy-start.11
  73.3 4.7 copy-start.1
  73.3 84.9 %all-to-all-start.1 = ((f32[8,32,32,128]{3,1,2,0:T(8,128)}), f32[8,32,32,128]{3,1,2,0:T(8,128)}, u32[]{:S(2)}, u32[]{:S(2)}) async-start(f32[8,32,32,128]{3,1,2,0:T(8,128)} %copy.71), calls=%async_computation.1 | async-start | bytes 8388608 | tf_op jit(solution)/shard_map/all_to_all | solution.py:125
  78.0 248.8 %all-gather.11.cloned.1.call-start = ((), (), s32[]{:S(2)}) async-start(), calls=%async_computation.5 | async-start | bytes 10485760 | tf_op jit(solution)/shard_map/all_gather | solution.py:133
  176.6 1.4 copy-start.8
  178.0 298.2 %all-gather.9.cloned.1.call-start = ((), (), s32[]{:S(2)}) async-start(), calls=%async_computation.4 | async-start | bytes 10485760 | tf_op jit(solution)/shard_map/all_gather | solution.py:133
  250.6 1.3 copy-start.9
  251.9 264.2 %all-gather.13.cloned.1.call-start = ((), (), s32[]{:S(2)}) async-start(), calls=%async_computation.6 | async-start | bytes 2359296 | tf_op jit(solution)/shard_map/all_gather | solution.py:142
  331.2 150.7 %copy-start.4 = (f32[2,16,64,256]{3,2,1,0:T(8,128)}, f32[2,16,64,256]{3,2,1,0:T(8,128)S(1)}, u32[]{:S(2)}) copy-start(f32[2,16,64,256]{3,2,1,0:T(8,128)S(1)} %reduce_sum.121) | copy-start | bytes 6291460
  487.7 1.3 copy-start.6
  490.0 267.3 %all-gather.15.cloned.1.call-start = ((), (), s32[]{:S(2)}) async-start(), calls=%async_computation.7 | async-start | bytes 10485760 | tf_op jit(solution)/shard_map/all_gather | solution.py:133
  519.4 1.7 copy-start.12
  608.1 1.3 copy-start.7
  609.4 153.6 %copy-start.5 = (f32[2,16,64,256]{3,2,1,0:T(8,128)S(1)}, f32[2,16,64,256]{3,2,1,0:T(8,128)}, u32[]{:S(2)}) copy-start(f32[2,16,64,256]{3,2,1,0:T(8,128)} %copy-done.4) | copy-start | bytes 6291460
Sparse Core Ops, SparseCore 0:
  14.2 30.4 all-gather.6
  178.1 148.6 all-gather.10
  328.4 147.7 all-gather.8
  490.1 25.9 all-gather.12
  609.5 147.7 all-gather.14
